TPU v7x, 128 devices: a whole 4x4x4 slice. The times are simulated.
128 devices in a mesh: req: 32 (over z, x, core), tp: 4 (over y).
Axes of the slice: x: 4, y: 4, z: 4, core: 2. Of those that a mesh axis runs over, the one named last changes fastest.
Arguments:
- tokens: bfloat16 [16384, 2560], P('req'), may hold values from -6 to 6
- lengths: int32 [32], P('req'), may hold values from 1 to 512, as said below
- page_slot: int32 [128], replicated, may hold values from 0 to 127, as said below
- trainer_layout: int32 [128], replicated, may hold values from 0 to 127, each once
- trainer_qkv: float32 [2560, 3840], P(('req', 'tp'))
- trainer_gateup: float32 [2560, 13824], P(('req', 'tp')), may hold values from -0.125 to 0.125
- attn_gain: float32 [2560], replicated, may hold values from 0.1 to 1.9
- ffn_gain: float32 [2560], replicated, may hold values from 0.1 to 1.9
- out_proj: bfloat16 [2560, 2560], P('tp'), may hold values from -0.125 to 0.125
- down_proj: bfloat16 [6912, 2560], P('tp'), may hold values from -0.078125 to 0.078125
Outputs:
- layer_out: bfloat16 [16384, 2560], P(('req', 'tp'))
- kv_cache: bfloat16 [128, 128, 1280], P('req', None, 'tp')
Inputs may be any that keep to these rules, and one draw needn't show every extreme that they name: `lengths`: heavy-tailed; some request has exactly 512. `page_slot`: a permutation; pool slot s belongs to request device s // 4; the 4 pages of one request belong to 4 different devices. `trainer_layout`: a permutation; shard s is the trainer shard on the device with index s over req and tp together.
All inputs are finite; a program needn't handle non-finite values.
Results may differ from a plain program's by a relative error of at most 0.0065.
The roundings to bfloat16 on the way count: a program that leaves them out, or rounds other values in their place, can miss the bound.
Values may be sent and summed in bfloat16 or wider, within the bound.
A program may use at most 192 MiB of HBM per device.

v0:
```python
import jax
import jax.numpy as jnp
from jax import lax
from jax.sharding import PartitionSpec as P

HD = 80
PAGE = 128
eps_norm = 1e-05
theta_base = 10000.0


def normed(values, gain):
    scale = lax.rsqrt(jnp.mean(values * values, axis=-1, keepdims=True) + eps_norm)
    return (values * scale * gain).astype(jnp.bfloat16)


def rotary(field, head_dim):
    half = head_dim // 2
    count = field.shape[0]
    freq = theta_base ** (-jnp.arange(half, dtype=jnp.float32) * 2.0 / head_dim)
    angles = jnp.arange(count, dtype=jnp.float32)[:, None] * freq[None, :]
    cosine = jnp.cos(angles)[:, None, :]
    sine = jnp.sin(angles)[:, None, :]
    first = field[..., :half]
    second = field[..., half:]
    return jnp.concatenate(
        [first * cosine - second * sine, second * cosine + first * sine], axis=-1
    )


def body(
    tokens,
    lengths,
    page_slot,
    trainer_layout,
    trainer_qkv,
    trainer_gateup,
    attn_gain,
    ffn_gain,
    out_proj,
    down_proj,
):
    n_tp = lax.axis_size("tp")
    n_req = lax.axis_size("req")
    devices = n_tp * n_req
    rows_each = trainer_qkv.shape[0]
    seq_len = tokens.shape[0]
    model_dim = tokens.shape[1]
    head_dim = HD
    local_heads = out_proj.shape[0] // head_dim
    group_cols = trainer_qkv.shape[1] // n_tp
    local_kv = (group_cols // head_dim - local_heads) // 2
    group = local_heads // local_kv
    q_cols = local_heads * head_dim
    k_cols = local_kv * head_dim
    ff_local = down_proj.shape[0]
    qkv_half, gu_half = (
        lax.all_to_all(
            trainer_qkv.astype(jnp.bfloat16), "tp", split_axis=1, concat_axis=0, tiled=True
        ),
        lax.all_to_all(
            trainer_gateup.astype(jnp.bfloat16), "tp", split_axis=1, concat_axis=0, tiled=True
        ),
    )
    x_f = tokens.astype(jnp.float32)
    x_norm = normed(x_f, attn_gain)
    inverse = (
        jnp.zeros((devices,), jnp.int32)
        .at[trainer_layout]
        .set(jnp.arange(devices, dtype=jnp.int32))
    )
    qkv_all, gu_all = (
        lax.all_gather(qkv_half, "req", axis=0, tiled=True),
        lax.all_gather(gu_half, "req", axis=0, tiled=True),
    )
    qkv_weight = qkv_all.reshape(devices, rows_each, qkv_all.shape[1])[inverse].reshape(
        model_dim, qkv_all.shape[1]
    )
    gu_weight = gu_all.reshape(devices, rows_each, gu_all.shape[1])[inverse].reshape(
        model_dim, gu_all.shape[1]
    )
    joined = jnp.dot(x_norm, qkv_weight, preferred_element_type=jnp.float32)
    query = rotary(joined[:, :q_cols].reshape(seq_len, local_heads, head_dim), head_dim)
    keys = rotary(
        joined[:, q_cols : q_cols + k_cols].reshape(seq_len, local_kv, head_dim), head_dim
    )
    query16 = query.astype(jnp.bfloat16).reshape(seq_len, local_kv, group, head_dim)
    keys16 = keys.astype(jnp.bfloat16)
    values16 = (
        joined[:, q_cols + k_cols :].reshape(seq_len, local_kv, head_dim).astype(jnp.bfloat16)
    )
    scores = jnp.einsum(
        "qkgd,skd->kgqs", query16, keys16, preferred_element_type=jnp.float32
    ) * head_dim ** (-0.5)
    slots = jnp.arange(seq_len, dtype=jnp.int32)
    length = lengths[0]
    allowed = (slots[None, :] <= slots[:, None]) & (slots[None, :] < length)
    scores = jnp.where(allowed[None, None], scores, -1e30)
    probs = jax.nn.softmax(scores, axis=-1).astype(jnp.bfloat16)
    context = jnp.einsum(
        "kgqs,skd->qkgd", probs, values16, preferred_element_type=jnp.float32
    ).astype(jnp.bfloat16)
    partial_out = jnp.dot(
        context.reshape(seq_len, q_cols), out_proj, preferred_element_type=jnp.float32
    )
    share = seq_len // n_tp
    tp_index = lax.axis_index("tp")
    mixed = lax.psum(partial_out, "tp")
    resid = x_f + mixed
    h_norm = normed(resid, ffn_gain)
    resid_share = lax.dynamic_slice_in_dim(resid, tp_index * share, share, 0)
    projected = jnp.dot(h_norm, gu_weight, preferred_element_type=jnp.float32)
    hidden = (jax.nn.silu(projected[:, :ff_local]) * projected[:, ff_local:]).astype(jnp.bfloat16)
    down = jnp.dot(hidden, down_proj, preferred_element_type=jnp.float32)
    added = lax.psum_scatter(down, "tp", scatter_dimension=0, tiled=True)
    share_slots = tp_index * share + jnp.arange(share, dtype=jnp.int32)
    live_share = (share_slots < length).astype(jnp.float32)
    layer_out = ((resid_share + added) * live_share[:, None]).astype(jnp.bfloat16)
    live_rows = (slots < length)[:, None]
    key_rows = keys16.reshape(seq_len, k_cols)
    value_rows = values16.reshape(seq_len, k_cols)
    cache_rows = jnp.concatenate(
        [
            jnp.where(live_rows, key_rows, jnp.zeros_like(key_rows)),
            jnp.where(live_rows, value_rows, jnp.zeros_like(value_rows)),
        ],
        axis=1,
    )
    pages = cache_rows.reshape(seq_len // PAGE, PAGE, 2 * k_cols)
    pool_size = pages.shape[0]
    owner = lax.axis_index("req")
    targets = owner * pool_size + jnp.arange(pool_size, dtype=jnp.int32)
    picks = (page_slot[:, None] == targets[None, :]).astype(jnp.bfloat16)
    pool = jnp.einsum(
        "np,nsc->psc",
        picks,
        lax.all_gather(pages, "req", axis=0, tiled=True),
        preferred_element_type=jnp.float32,
    )
    kv_cache = pool.astype(jnp.bfloat16)
    return (layer_out, kv_cache)


def solution(mesh):
    return jax.shard_map(
        body,
        mesh=mesh,
        in_specs=(
            P("req", None),
            P("req"),
            P(),
            P(),
            P(("req", "tp"), None),
            P(("req", "tp"), None),
            P(),
            P(),
            P("tp", None),
            P("tp", None),
        ),
        out_specs=(P(("req", "tp"), None), P("req", None, "tp")),
        check_vma=False,
    )
```

profile of v0, /device:TPU:1, one launch (start us, length us, event | category | flops | bytes accessed | tf_op | source)
XLA Modules:
  0.0 472.2 jit_solution(814724774709201183)
XLA Ops:
  7.2 0.0 copy-start
  7.2 0.0 all-gather.4.cloned.1.call-start
  7.2 1.2 convert_element_type.60
  8.4 0.9 all_to_all.28
  9.3 1.0 copy.18
  10.3 10.0 %all_to_all.38 = bf16[20,4,960]{2,0,1:T(8,128)(2,1)S(1)} all-to-all(bf16[20,4,960]{2,0,1:T(8,128)(2,1)S(1)} %copy.18), channel_id=1, replica_groups=mesh['req'=32,'tp'=4] {'tp'}, dimensions={1} | all-to-all | bytes 307200 | tf_op jit(solution)/shard_map/all_to_all | solution.py:58
  20.3 0.7 all_to_all.31
  21.0 0.0 all-gather.4.cloned.1.call-update
  21.0 0.0 all-reduce.2.cloned.1.call-start
  21.7 0.7 compare_select_fusion.1
  22.4 1.0 scatter_custom_fusion
  23.4 2.3 fusion.4
  25.8 0.4 fusion.35
  26.1 0.8 fusion.26
  27.0 43.9 %all-gather.4.cloned.1.call-done = bf16[2560,960]{1,0:T(8,128)(2,1)} async-done(((bf16[80,960]{1,0:T(8,128)(2,1)}), bf16[2560,960]{1,0:T(8,128)(2,1)}) %all-gather.4.cloned.1.call-update) | async-done | bytes 4915216 | tf_op jit(solution)/shard_map/all_gather | solution.py:73
  70.9 9.7 %reshape.159 = bf16[128,20,960]{2,1,0:T(8,128)(2,1)} reshape(bf16[2560,960]{1,0:T(8,128)(2,1)} %all-gather.4.cloned.1.call-done) | data formatting | bytes 9830400 | tf_op jit(solution)/shard_map/reshape | solution.py:76
  80.6 6.4 %gather_fusion = bf16[128,20,960]{2,1,0:T(8,128)(2,1)} fusion(bf16[128,20,960]{2,1,0:T(8,128)(2,1)} %reshape.159, s32[1024]{0:T(1024)S(1)} %pad_clamp_fusion), kind=kCustom, calls=%fused_computation | custom fusion | bytes 9830912 | tf_op jit(solution)/shard_map/gather | solution.py:76
  87.0 0.0 copy-start.7
  87.0 9.8 %reshape.160 = bf16[2560,960]{1,0:T(8,128)(2,1)} reshape(bf16[128,20,960]{2,1,0:T(8,128)(2,1)} %gather_fusion) | data formatting | bytes 9830400 | tf_op jit(solution)/shard_map/reshape | solution.py:76
  96.8 0.0 copy-done.7
  96.8 6.2 %fusion.13 = f32[512,960]{0,1:T(8,128)S(1)} fusion(bf16[2560,960]{1,0:T(8,128)(2,1)} %reshape.160, bf16[512,2560]{1,0:T(8,128)(2,1)} %param.10, f32[2560]{0:T(1024)S(1)} %copy-done.7, f32[512]{0:T(512)S(1)} %add_rsqrt_fusion.1), kind=kOutput, calls=%fused_computation.25 | convolution fusion | flops 2521825280 | bytes 9515008 | tf_op jit(solution)/shard_map/dot_general | solution.py:82
  103.0 0.8 select_bitcast_fusion
  103.8 0.1 slice.44
  103.9 1.0 subtract_convert_fusion
  104.9 0.7 multiply_subtract_fusion
  105.6 7.6 %fusion.49 = (f32[2,4,512]{2,1,0:T(4,128)S(1)}, f32[2,4,512,512]{2,3,1,0:T(8,128)}) fusion(pred[512,512]{0,1:T(8,128)(4,1)} %fusion.26, bf16[512,2,4,40]{0,3,2,1:T(8,128)(2,1)} %bitcast.65, bf16[512,2,4,40]{0,3,2,1:T(8,128)(2,1)} %bitcast.64, bf16[512,2,40]{0,2,1:T(8,128)(2,1)} %get-tuple-element.15, bf16[512,2,40]{0,2,1:T(8,128)(2,1)S(1)} %get-tuple-element.14), kind=kOutput, calls=%fused_computation.76 | convolution fusion | flops 345571840 | bytes 9486336 | tf_op jit(solution)/shard_map/sub | solution.py:99
  113.2 0.0 copy-done.5
  113.2 4.2 fusion.22
  117.4 0.0 copy-done
  117.4 4.6 fusion.54
  122.0 0.0 all-reduce.2.cloned.1.call-update
  122.0 0.0 copy-start.2
  122.1 0.0 all-gather.6.cloned.1.call-start
  122.1 2.4 convert_element_type.68
  124.5 1.3 all_to_all.32
  125.8 0.1 copy.20
  125.9 21.6 %all_to_all.39 = bf16[20,4,3456]{2,0,1:T(8,128)(2,1)} all-to-all(bf16[20,4,3456]{2,0,1:T(8,128)(2,1)S(1)} %copy.20), channel_id=1, replica_groups=mesh['req'=32,'tp'=4] {'tp'}, dimensions={1} | all-to-all | bytes 1105920 | tf_op jit(solution)/shard_map/all_to_all | solution.py:61
  147.5 2.0 all_to_all.35
  149.5 0.0 all-gather.6.cloned.1.call-update
  149.6 0.2 all-gather.8.cloned.1.call-start
  149.8 0.0 copy-done.3
  149.9 0.0 copy-done.4
  150.0 0.7 pad_maximum_fusion.7
  150.7 0.0 all-gather.8.cloned.1.call-update
  150.8 0.0 reduce-scatter.2.cloned.1.call-start
  150.8 86.5 %all-reduce.2.cloned.1.call-done = f32[512,2560]{1,0:T(8,128)} async-done(((f32[512,2560]{1,0:T(8,128)}), f32[512,2560]{1,0:T(8,128)}) %all-reduce.2.cloned.1.call-update) | async-done | bytes 5242896 | tf_op jit(solution)/shard_map/psum | solution.py:108
  237.3 0.0 copy-done.2
  237.4 5.4 %multiply_reduce_fusion = (f32[512]{0:T(512)S(1)}, f32[512,2560]{1,0:T(8,128)}) fusion(f32[512,2560]{1,0:T(8,128)} %all-reduce.2.cloned.1.call-done, bf16[512,2560]{1,0:T(8,128)(2,1)S(1)} %copy-done.2), kind=kLoop, calls=%fused_computation.17 | loop fusion | flops 5242368 | bytes 13109248 | tf_op jit(solution)/shard_map/reduce_sum | solution.py:13
  242.8 72.6 %all-gather.6.cloned.1.call-done = bf16[2560,3456]{1,0:T(8,128)(2,1)} async-done(((bf16[80,3456]{1,0:T(8,128)(2,1)}), bf16[2560,3456]{1,0:T(8,128)(2,1)}) %all-gather.6.cloned.1.call-update) | async-done | bytes 17694736 | tf_op jit(solution)/shard_map/all_gather | solution.py:74
  315.4 24.5 %reshape.164 = bf16[128,20,3456]{2,1,0:T(8,128)(2,1)} reshape(bf16[2560,3456]{1,0:T(8,128)(2,1)} %all-gather.6.cloned.1.call-done) | data formatting | bytes 35389440 | tf_op jit(solution)/shard_map/reshape | solution.py:79
  339.9 17.0 %gather_fusion.1 = bf16[128,20,3456]{2,1,0:T(8,128)(2,1)} fusion(bf16[128,20,3456]{2,1,0:T(8,128)(2,1)} %reshape.164, s32[1024]{0:T(1024)S(1)} %pad_clamp_fusion), kind=kCustom, calls=%fused_computation.1 | custom fusion | bytes 35389952 | tf_op jit(solution)/shard_map/gather | solution.py:79
  356.9 25.1 %reshape.165 = bf16[2560,3456]{1,0:T(8,128)(2,1)} reshape(bf16[128,20,3456]{2,1,0:T(8,128)(2,1)} %gather_fusion.1) | data formatting | bytes 35389440 | tf_op jit(solution)/shard_map/reshape | solution.py:79
  382.0 0.0 copy-done.8
  382.0 15.3 %fusion.12 = f32[512,3456]{1,0:T(8,128)S(1)} fusion(bf16[2560,3456]{1,0:T(8,128)(2,1)} %reshape.165, f32[512,2560]{1,0:T(8,128)} %get-tuple-element.11, f32[2560]{0:T(1024)S(1)} %copy-done.8, f32[512]{0:T(512)S(1)} %add_rsqrt_fusion), kind=kOutput, calls=%fused_computation.24 | convolution fusion | flops 9063628800 | bytes 30027776 | tf_op jit(solution)/shard_map/dot_general | solution.py:112
  397.3 10.4 %fusion.19 = f32[512,2560]{1,0:T(8,128)} fusion(bf16[1728,2560]{1,0:T(8,128)(2,1)} %param.19, f32[512,3456]{1,0:T(8,128)S(1)} %fusion.12), kind=kOutput, calls=%fused_computation.30 | convolution fusion | flops 4535156736 | bytes 21430272 | tf_op jit(solution)/shard_map/dot_general | solution.py:114
  407.7 0.0 reduce-scatter.2.cloned.1.call-update
  407.8 0.0 copy-start.1
  407.8 0.0 all-gather.8.cloned.1.call-done
  407.8 0.6 copy-done.6
  408.4 9.9 %fusion.23 = bf16[4,128,320]{1,0,2:T(4,128)(2,1)S(1)} fusion(bf16[128,128,320]{1,2,0:T(8,128)(2,1)} %all-gather.8.cloned.1.call-done, s32[128]{0:T(128)S(1)} %copy-done.6, s32[4]{0:T(128)S(1)} %iota_add_fusion), kind=kOutput, calls=%fused_computation.34 | convolution fusion | flops 42107392 | bytes 10813968 | tf_op jit(solution)/shard_map/np,nsc->psc/dot_general | solution.py:134
  418.3 0.8 copy.24
  419.1 43.9 %reduce-scatter.2.cloned.1.call-done = f32[128,2560]{1,0:T(8,128)} async-done(((f32[512,2560]{1,0:T(8,128)}), f32[128,2560]{1,0:T(8,128)}) %reduce-scatter.2.cloned.1.call-update) | async-done | bytes 1310736 | tf_op jit(solution)/shard_map/reduce_scatter | solution.py:115
  462.9 2.7 multiply_convert_fusion.2
  465.6 0.0 copy-done.1
  (20 shorter events, 0.2 us)
Async XLA Ops:
  7.2 110.3 %copy-start = (bf16[640,2560]{1,0:T(8,128)(2,1)S(1)}, bf16[640,2560]{1,0:T(8,128)(2,1)}, u32[]{:S(2)}) copy-start(bf16[640,2560]{1,0:T(8,128)(2,1)} %param.18) | copy-start | bytes 9830404
  7.2 63.7 %all-gather.4.cloned.1.call-start = ((), (), s32[]{:S(2)}) async-start(), calls=%async_computation.3 | async-start | bytes 5406720 | tf_op jit(solution)/shard_map/all_gather | solution.py:73
  21.0 216.3 %all-reduce.2.cloned.1.call-start = ((), (), s32[]{:S(2)}) async-start(), calls=%async_computation.4 | async-start | bytes 10485760 | tf_op jit(solution)/shard_map/psum | solution.py:108
  87.0 9.8 %copy-start.7 = (f32[2560]{0:T(1024)S(1)}, f32[2560]{0:T(1024)}, u32[]{:S(2)}) copy-start(f32[2560]{0:T(1024)} %param.16) | copy-start | bytes 30724
  105.6 7.6 %copy-start.5 = (bf16[512,160]{0,1:T(8,128)(2,1)S(1)}, bf16[512,160]{0,1:T(8,128)(2,1)}, u32[]{:S(2)}) copy-start(bf16[512,160]{0,1:T(8,128)(2,1)} %get-tuple-element.9) | copy-start | bytes 491524
  122.0 27.8 %copy-start.3 = (bf16[20,4,8,128]{3,2,1,0:T(8,128)(2,1)S(1)}, bf16[20,4,8,128]{3,2,1,0:T(8,128)(2,1)}, u32[]{:S(2)}) copy-start(bf16[20,4,8,128]{3,2,1,0:T(8,128)(2,1)} %get-tuple-element.8) | copy-start | bytes 491524
  122.0 27.8 %copy-start.4 = (bf16[512,2,40]{0,2,1:T(8,128)(2,1)S(1)}, bf16[512,2,40]{0,2,1:T(8,128)(2,1)}, u32[]{:S(2)}) copy-start(bf16[512,2,40]{0,2,1:T(8,128)(2,1)} %get-tuple-element.15) | copy-start | bytes 245764
  122.0 115.3 %copy-start.2 = (bf16[512,2560]{1,0:T(8,128)(2,1)S(1)}, bf16[512,2560]{1,0:T(8,128)(2,1)}, u32[]{:S(2)}) copy-start(bf16[512,2560]{1,0:T(8,128)(2,1)} %param.10) | copy-start | bytes 7864324
  122.1 193.3 %all-gather.6.cloned.1.call-start = ((), (), s32[]{:S(2)}) async-start(), calls=%async_computation.5 | async-start | bytes 18247680 | tf_op jit(solution)/shard_map/all_gather | solution.py:74
  149.6 258.2 %all-gather.8.cloned.1.call-start = ((), (), s32[]{:S(2)}) async-start(), calls=%async_computation.7 | async-start | bytes 10813440 | tf_op jit(solution)/shard_map/all_gather | solution.py:137
  150.8 312.2 %reduce-scatter.2.cloned.1.call-start = ((), (), s32[]{:S(2)}) async-start(), calls=%async_computation.6 | async-start | bytes 6553600 | tf_op jit(solution)/shard_map/reduce_scatter | solution.py:115
  356.9 25.1 %copy-start.8 = (f32[2560]{0:T(1024)S(1)}, f32[2560]{0:T(1024)}, u32[]{:S(2)}) copy-start(f32[2560]{0:T(1024)} %param.17) | copy-start | bytes 30724
  407.7 0.7 copy-start.6
  407.8 57.9 %copy-start.1 = (bf16[640,2560]{1,0:T(8,128)(2,1)S(1)}, bf16[640,2560]{1,0:T(8,128)(2,1)}, u32[]{:S(2)}) copy-start(bf16[640,2560]{1,0:T(8,128)(2,1)} %param.18) | copy-start | bytes 9830404
Sparse Core Ops, SparseCore 0:
  21.1 49.7 all-gather.3
  122.2 115.1 all-reduce.1
  240.3 75.0 all-gather.5
  318.1 57.3 all-gather.7
  407.9 55.0 reduce-scatter.1
where the time goes:
time: 474 us; the launch traced here: 472 us
  waiting for transfers between devices  247 us (52%)
  local copies, waits for them, and re-layouts  101 us (21%)
  matrix products  58.2 us (12%)
  blocking collectives  31.6 us (7%)
  other arithmetic  19.2 us (4%)
  between operations  14.6 us (3%)
    psum x1, waiting for transfers between devices, body(): mixed = lax.psum(partial_out, 'tp')  86.5 us
    all_gather x1, waiting for transfers between devices, body(): lax.all_gather(gu_half, 'req', axis=0, tiled=True)  72.6 us
    reshape x2, local copies, waits for them, and re-layouts, body(): gu_all.reshape(devices, rows_each, gu_all.shape[1])[inverse]  49.7 us
    all_gather x1, waiting for transfers between devices, body(): lax.all_gather(qkv_half, 'req', axis=0, tiled=True)  43.9 us
    reduce_scatter x1, waiting for transfers between devices, body(): added = lax.psum_scatter(down, 'tp', scatter_dimension=0, tiled=True)  43.9 us
    all_to_all x1, blocking collectives, body(): lax.all_to_all(trainer_gateup.astype(jnp.bfloat16), 'tp', split_axis=1, c...  21.6 us
    reshape x2, local copies, waits for them, and re-layouts, body(): qkv_all.reshape(devices, rows_each, qkv_all.shape[1])[inverse]  19.5 us
    gather x1, local copies, waits for them, and re-layouts, body(): gu_all.reshape(devices, rows_each, gu_all.shape[1])[inverse]  17 us
  transfers between devices with their start and end apart: 5, of which 4 were waited for; matrix products, arithmetic and copies ran while one was open for 25% of the time, Pallas kernels for 0%

commit v1 on v0

--- a/solution.py
+++ b/solution.py
@@ -7,6 +7,29 @@
 PAGE = 128
 eps_norm = 1e-05
 theta_base = 10000.0
+
+
+def in_blocks(x, dim, devices):
+    shape = x.shape
+    tiles = x.reshape(*shape[:dim], devices, shape[dim] // devices, *shape[dim + 1 :])
+    return jnp.moveaxis(tiles, dim, 0)
+
+
+def laid_out(blocks, dim):
+    lengths = list(blocks.shape[1:])
+    lengths[dim] *= blocks.shape[0]
+    return jnp.moveaxis(blocks, 0, dim).reshape(lengths)
+
+
+def exchange_in_pairs(shard, axis, split_dim, concat_dim):
+    size, index = (lax.axis_size(axis), lax.axis_index(axis))
+    blocks = in_blocks(shard, split_dim, size)
+    gathered = [blocks[index]]
+    for step in range(1, size):
+        sent = blocks[index ^ step]
+        gathered.append(lax.ppermute(sent, axis, [(i, i ^ step) for i in range(size)]))
+    blocks = jnp.stack(gathered)[index ^ jnp.arange(size)]
+    return laid_out(blocks, concat_dim)
 
 
 def normed(values, gain):
@@ -55,9 +78,7 @@
     k_cols = local_kv * head_dim
     ff_local = down_proj.shape[0]
     qkv_half, gu_half = (
-        lax.all_to_all(
-            trainer_qkv.astype(jnp.bfloat16), "tp", split_axis=1, concat_axis=0, tiled=True
-        ),
+        exchange_in_pairs(trainer_qkv.astype(jnp.bfloat16), "tp", 1, 0),
         lax.all_to_all(
             trainer_gateup.astype(jnp.bfloat16), "tp", split_axis=1, concat_axis=0, tiled=True
         ),

time: 474 us -> 476 us (level)
  blocking collectives: 31.6 us -> 21.6 us
  waiting for transfers between devices: 247 us -> 252 us
    all_to_all x1 -> x0, blocking collectives: 9.99 us -> none  [body(): lax.all_to_all(trainer_qkv.astype(jnp.bfloat16), 'tp', split_axis=1, conc...]
  transfers between devices with their start and end apart: 5 -> 8, of which waited for: 4 -> 6; matrix products, arithmetic and copies ran while one was open for 25% -> 25% of each run, Pallas kernels for 0% -> 0%
where the time goes in v1:
time: 476 us; the launch traced here: 474 us
  waiting for transfers between devices  252 us (53%)
  local copies, waits for them, and re-layouts  103 us (22%)
  matrix products  58.2 us (12%)
  blocking collectives  21.6 us (5%)
  other arithmetic  19.9 us (4%)
  between operations  14.7 us (3%)
  starting transfers between devices  4.82 us (1%)
    psum x1, waiting for transfers between devices, body(): mixed = lax.psum(partial_out, 'tp')  86.5 us
    all_gather x1, waiting for transfers between devices, body(): lax.all_gather(gu_half, 'req', axis=0, tiled=True)  72.6 us
    reshape x2, local copies, waits for them, and re-layouts, body(): gu_all.reshape(devices, rows_each, gu_all.shape[1])[inverse]  49.7 us
    all_gather x1, waiting for transfers between devices, body(): lax.all_gather(qkv_half, 'req', axis=0, tiled=True)  44.7 us
    reduce_scatter x1, waiting for transfers between devices, body(): added = lax.psum_scatter(down, 'tp', scatter_dimension=0, tiled=True)  43.9 us
    all_to_all x1, blocking collectives, body(): lax.all_to_all(trainer_gateup.astype(jnp.bfloat16), 'tp', split_axis=1, c...  21.6 us
    reshape x2, local copies, waits for them, and re-layouts, body(): qkv_all.reshape(devices, rows_each, qkv_all.shape[1])[inverse]  19.5 us
    gather x1, local copies, waits for them, and re-layouts, body(): gu_all.reshape(devices, rows_each, gu_all.shape[1])[inverse]  17 us
  transfers between devices with their start and end apart: 8, of which 6 were waited for; matrix products, arithmetic and copies ran while one was open for 25% of the time, Pallas kernels for 0%

profile of v1, /device:TPU:1, one launch (start us, length us, event | category | flops | bytes accessed | tf_op | source)
XLA Modules:
  0.0 474.0 jit_solution(2891430676380902186)
XLA Ops:
  7.2 0.0 copy-start
  7.2 0.0 all-gather.4.cloned.1.call-start
  7.2 1.8 convert_element_type.60
  9.1 1.2 reshape.185
  10.3 0.3 constant_dynamic-slice_fusion.3
  10.6 3.6 collective-permute-start.2
  14.3 0.4 collective-permute-start.1
  14.8 0.3 collective-permute-start
  15.1 0.6 collective-permute-done.2
  15.8 3.1 collective-permute-done.1
  18.8 0.0 collective-permute-done
  18.9 1.2 gather_fusion
  20.1 1.6 reshape.186
  21.8 0.0 all-gather.4.cloned.1.call-update
  21.8 0.0 all-reduce.2.cloned.1.call-start
  22.5 0.7 compare_select_fusion.1
  23.1 1.2 scatter_custom_fusion
  24.4 2.3 fusion.4
  26.7 0.4 fusion.35
  27.1 0.9 fusion.26
  27.9 44.7 %all-gather.4.cloned.1.call-done = bf16[2560,960]{1,0:T(8,128)(2,1)} async-done(((bf16[80,960]{1,0:T(8,128)(2,1)}), bf16[2560,960]{1,0:T(8,128)(2,1)}) %all-gather.4.cloned.1.call-update) | async-done | bytes 4915216 | tf_op jit(solution)/shard_map/all_gather | solution.py:94
  72.6 9.7 %reshape.187 = bf16[128,20,960]{2,1,0:T(8,128)(2,1)} reshape(bf16[2560,960]{1,0:T(8,128)(2,1)} %all-gather.4.cloned.1.call-done) | data formatting | bytes 9830400 | tf_op jit(solution)/shard_map/reshape | solution.py:97
  82.4 6.4 %gather_fusion.1 = bf16[128,20,960]{2,1,0:T(8,128)(2,1)} fusion(bf16[128,20,960]{2,1,0:T(8,128)(2,1)} %reshape.187, s32[1024]{0:T(1024)S(1)} %pad_clamp_fusion), kind=kCustom, calls=%fused_computation.1 | custom fusion | bytes 9830912 | tf_op jit(solution)/shard_map/gather | solution.py:97
  88.7 9.8 %reshape.188 = bf16[2560,960]{1,0:T(8,128)(2,1)} reshape(bf16[128,20,960]{2,1,0:T(8,128)(2,1)} %gather_fusion.1) | data formatting | bytes 9830400 | tf_op jit(solution)/shard_map/reshape | solution.py:97
  98.5 6.2 %fusion.13 = f32[512,960]{0,1:T(8,128)S(1)} fusion(bf16[2560,960]{1,0:T(8,128)(2,1)} %reshape.188, bf16[512,2560]{1,0:T(8,128)(2,1)} %param.10, f32[2560]{0:T(1024)S(1)} %copy-done.7, f32[512]{0:T(512)S(1)} %add_rsqrt_fusion.1), kind=kOutput, calls=%fused_computation.26 | convolution fusion | flops 2521825280 | bytes 9515008 | tf_op jit(solution)/shard_map/dot_general | solution.py:103
  104.7 0.7 select_bitcast_fusion
  105.4 0.1 slice.46
  105.6 1.0 subtract_convert_fusion
  106.6 0.7 multiply_subtract_fusion
  107.3 7.6 %fusion.50 = (f32[2,4,512]{2,1,0:T(4,128)S(1)}, f32[2,4,512,512]{2,3,1,0:T(8,128)}) fusion(pred[512,512]{0,1:T(8,128)(4,1)} %fusion.26, bf16[512,2,4,40]{0,3,2,1:T(8,128)(2,1)} %bitcast.80, bf16[512,2,4,40]{0,3,2,1:T(8,128)(2,1)} %bitcast.79, bf16[512,2,40]{0,2,1:T(8,128)(2,1)} %get-tuple-element.17, bf16[512,2,40]{0,2,1:T(8,128)(2,1)S(1)} %get-tuple-element.16), kind=kOutput, calls=%fused_computation.89 | convolution fusion | flops 345571840 | bytes 9486336 | tf_op jit(solution)/shard_map/sub | solution.py:120
  114.9 4.2 fusion.22
  119.1 4.6 fusion.55
  123.7 0.0 all-reduce.2.cloned.1.call-update
  123.7 0.0 copy-start.2
  123.8 0.0 all-gather.6.cloned.1.call-start
  123.8 2.4 convert_element_type.68
  126.2 1.3 all_to_all.14
  127.5 0.1 copy.21
  127.6 21.6 %all_to_all.19 = bf16[20,4,3456]{2,0,1:T(8,128)(2,1)} all-to-all(bf16[20,4,3456]{2,0,1:T(8,128)(2,1)S(1)} %copy.21), channel_id=1, replica_groups=mesh['req'=32,'tp'=4] {'tp'}, dimensions={1} | all-to-all | bytes 1105920 | tf_op jit(solution)/shard_map/all_to_all | solution.py:82
  149.2 2.0 all_to_all.17
  151.2 0.0 all-gather.6.cloned.1.call-update
  151.3 0.3 all-gather.8.cloned.1.call-start
  151.7 0.7 pad_maximum_fusion.7
  152.5 0.0 all-gather.8.cloned.1.call-update
  152.5 0.0 reduce-scatter.2.cloned.1.call-start
  152.5 86.5 %all-reduce.2.cloned.1.call-done = f32[512,2560]{1,0:T(8,128)} async-done(((f32[512,2560]{1,0:T(8,128)}), f32[512,2560]{1,0:T(8,128)}) %all-reduce.2.cloned.1.call-update) | async-done | bytes 5242896 | tf_op jit(solution)/shard_map/psum | solution.py:129
  239.1 0.0 copy-done.2
  239.1 5.4 %multiply_reduce_fusion = (f32[512]{0:T(512)S(1)}, f32[512,2560]{1,0:T(8,128)}) fusion(f32[512,2560]{1,0:T(8,128)} %all-reduce.2.cloned.1.call-done, bf16[512,2560]{1,0:T(8,128)(2,1)S(1)} %copy-done.2), kind=kLoop, calls=%fused_computation.18 | loop fusion | flops 5242368 | bytes 13109248 | tf_op jit(solution)/shard_map/reduce_sum | solution.py:36
  244.5 72.6 %all-gather.6.cloned.1.call-done = bf16[2560,3456]{1,0:T(8,128)(2,1)} async-done(((bf16[80,3456]{1,0:T(8,128)(2,1)}), bf16[2560,3456]{1,0:T(8,128)(2,1)}) %all-gather.6.cloned.1.call-update) | async-done | bytes 17694736 | tf_op jit(solution)/shard_map/all_gather | solution.py:95
  317.1 24.6 %reshape.192 = bf16[128,20,3456]{2,1,0:T(8,128)(2,1)} reshape(bf16[2560,3456]{1,0:T(8,128)(2,1)} %all-gather.6.cloned.1.call-done) | data formatting | bytes 35389440 | tf_op jit(solution)/shard_map/reshape | solution.py:100
  341.7 17.0 %gather_fusion.2 = bf16[128,20,3456]{2,1,0:T(8,128)(2,1)} fusion(bf16[128,20,3456]{2,1,0:T(8,128)(2,1)} %reshape.192, s32[1024]{0:T(1024)S(1)} %pad_clamp_fusion), kind=kCustom, calls=%fused_computation.2 | custom fusion | bytes 35389952 | tf_op jit(solution)/shard_map/gather | solution.py:100
  358.6 25.1 %reshape.193 = bf16[2560,3456]{1,0:T(8,128)(2,1)} reshape(bf16[128,20,3456]{2,1,0:T(8,128)(2,1)} %gather_fusion.2) | data formatting | bytes 35389440 | tf_op jit(solution)/shard_map/reshape | solution.py:100
  383.8 0.0 copy-done.8
  383.8 15.3 %fusion.12 = f32[512,3456]{1,0:T(8,128)S(1)} fusion(bf16[2560,3456]{1,0:T(8,128)(2,1)} %reshape.193, f32[512,2560]{1,0:T(8,128)} %get-tuple-element.13, f32[2560]{0:T(1024)S(1)} %copy-done.8, f32[512]{0:T(512)S(1)} %add_rsqrt_fusion), kind=kOutput, calls=%fused_computation.25 | convolution fusion | flops 9063628800 | bytes 30027776 | tf_op jit(solution)/shard_map/dot_general | solution.py:133
  399.1 10.4 %fusion.19 = f32[512,2560]{1,0:T(8,128)} fusion(bf16[1728,2560]{1,0:T(8,128)(2,1)} %param.19, f32[512,3456]{1,0:T(8,128)S(1)} %fusion.12), kind=kOutput, calls=%fused_computation.31 | convolution fusion | flops 4535156736 | bytes 21430272 | tf_op jit(solution)/shard_map/dot_general | solution.py:135
  409.6 0.0 reduce-scatter.2.cloned.1.call-update
  409.6 0.0 copy-start.1
  409.6 0.0 all-gather.8.cloned.1.call-done
  409.7 0.6 copy-done.6
  410.2 9.9 %fusion.23 = bf16[4,128,320]{1,0,2:T(4,128)(2,1)S(1)} fusion(bf16[128,128,320]{1,2,0:T(8,128)(2,1)} %all-gather.8.cloned.1.call-done, s32[128]{0:T(128)S(1)} %copy-done.6, s32[4]{0:T(128)S(1)} %iota_add_fusion), kind=kOutput, calls=%fused_computation.35 | convolution fusion | flops 42107392 | bytes 10813968 | tf_op jit(solution)/shard_map/np,nsc->psc/dot_general | solution.py:155
  420.1 0.8 copy.25
  420.9 43.9 %reduce-scatter.2.cloned.1.call-done = f32[128,2560]{1,0:T(8,128)} async-done(((f32[512,2560]{1,0:T(8,128)}), f32[128,2560]{1,0:T(8,128)}) %reduce-scatter.2.cloned.1.call-update) | async-done | bytes 1310736 | tf_op jit(solution)/shard_map/reduce_scatter | solution.py:136
  464.8 2.7 multiply_convert_fusion.2
  467.5 0.0 copy-done.1
  (33 shorter events, 0.3 us)
Async XLA Ops:
  7.2 112.0 %copy-start = (bf16[640,2560]{1,0:T(8,128)(2,1)S(1)}, bf16[640,2560]{1,0:T(8,128)(2,1)}, u32[]{:S(2)}) copy-start(bf16[640,2560]{1,0:T(8,128)(2,1)} %param.18) | copy-start | bytes 9830404
  7.2 65.4 %all-gather.4.cloned.1.call-start = ((), (), s32[]{:S(2)}) async-start(), calls=%async_computation.2 | async-start | bytes 5406720 | tf_op jit(solution)/shard_map/all_gather | solution.py:94
  10.6 5.1 %collective-permute-start.2 = (bf16[20,960]{1,0:T(8,128)(2,1)S(1)}, bf16[20,960]{1,0:T(8,128)(2,1)S(1)}, u32[]{:S(2)}, u32[]{:S(2)}) collective-permute-start(bf16[20,960]{1,0:T(8,128)(2,1)S(1)} %bitcast.86), channel_id=1, source_target_pairs={{0,3},{1,2},{2,1},{3,0},{4,7},{5,6},{6,5},{7,4},{8,11},{9,10},{10,... | collective-permute-start | bytes 115208 | tf_op jit(solution)/shard_map/ppermute | solution.py:30
  14.3 4.5 collective-permute-start.1
  14.8 4.1 collective-permute-start
  21.8 217.3 %all-reduce.2.cloned.1.call-start = ((), (), s32[]{:S(2)}) async-start(), calls=%async_computation.3 | async-start | bytes 10485760 | tf_op jit(solution)/shard_map/psum | solution.py:129
  88.7 9.8 %copy-start.7 = (f32[2560]{0:T(1024)S(1)}, f32[2560]{0:T(1024)}, u32[]{:S(2)}) copy-start(f32[2560]{0:T(1024)} %param.16) | copy-start | bytes 30724
  107.3 7.6 %copy-start.5 = (bf16[512,160]{0,1:T(8,128)(2,1)S(1)}, bf16[512,160]{0,1:T(8,128)(2,1)}, u32[]{:S(2)}) copy-start(bf16[512,160]{0,1:T(8,128)(2,1)} %get-tuple-element.11) | copy-start | bytes 491524
  123.7 27.8 %copy-start.3 = (bf16[20,4,8,128]{3,2,1,0:T(8,128)(2,1)S(1)}, bf16[20,4,8,128]{3,2,1,0:T(8,128)(2,1)}, u32[]{:S(2)}) copy-start(bf16[20,4,8,128]{3,2,1,0:T(8,128)(2,1)} %get-tuple-element.10) | copy-start | bytes 491524
  123.7 27.9 %copy-start.4 = (bf16[512,2,40]{0,2,1:T(8,128)(2,1)S(1)}, bf16[512,2,40]{0,2,1:T(8,128)(2,1)}, u32[]{:S(2)}) copy-start(bf16[512,2,40]{0,2,1:T(8,128)(2,1)} %get-tuple-element.17) | copy-start | bytes 245764
  123.7 115.3 %copy-start.2 = (bf16[512,2560]{1,0:T(8,128)(2,1)S(1)}, bf16[512,2560]{1,0:T(8,128)(2,1)}, u32[]{:S(2)}) copy-start(bf16[512,2560]{1,0:T(8,128)(2,1)} %param.10) | copy-start | bytes 7864324
  123.8 193.3 %all-gather.6.cloned.1.call-start = ((), (), s32[]{:S(2)}) async-start(), calls=%async_computation.4 | async-start | bytes 18247680 | tf_op jit(solution)/shard_map/all_gather | solution.py:95
  151.3 258.4 %all-gather.8.cloned.1.call-start = ((), (), s32[]{:S(2)}) async-start(), calls=%async_computation.6 | async-start | bytes 10813440 | tf_op jit(solution)/shard_map/all_gather | solution.py:158
  152.5 312.3 %reduce-scatter.2.cloned.1.call-start = ((), (), s32[]{:S(2)}) async-start(), calls=%async_computation.5 | async-start | bytes 6553600 | tf_op jit(solution)/shard_map/reduce_scatter | solution.py:136
  358.6 25.1 %copy-start.8 = (f32[2560]{0:T(1024)S(1)}, f32[2560]{0:T(1024)}, u32[]{:S(2)}) copy-start(f32[2560]{0:T(1024)} %param.17) | copy-start | bytes 30724
  409.6 0.7 copy-start.6
  409.6 57.9 %copy-start.1 = (bf16[640,2560]{1,0:T(8,128)(2,1)S(1)}, bf16[640,2560]{1,0:T(8,128)(2,1)}, u32[]{:S(2)}) copy-start(bf16[640,2560]{1,0:T(8,128)(2,1)} %param.18) | copy-start | bytes 9830404
Sparse Core Ops, SparseCore 0:
  21.9 50.6 all-gather.3
  123.9 115.1 all-reduce.1
  242.0 75.0 all-gather.5
  319.8 57.3 all-gather.7
  409.7 55.0 reduce-scatter.1
